TPU v7x, 32 devices: a whole 2x2x4 slice. The times are simulated.
32 devices in a mesh: region: 4 (over z), tracer: 2 (over x), sect: 4 (over y, core).
Axes of the slice: x: 2, y: 2, z: 4, core: 2. Of those that a mesh axis runs over, the one named last changes fastest.
Arguments:
- solute_concentration: float32 [16, 96, 32, 128], P('tracer', 'region', 'sect'), may hold values from 0.5 to 2
- thermal_anomaly: float32 [96, 32, 128], P('region', 'sect'), may hold values from -6 to 6
- eastward_flow_speed: float32 [96, 32, 128], P('region', 'sect'), may hold values from -1 to 1
- northward_flow_speed: float32 [96, 32, 128], P('region', 'sect'), may hold values from -1 to 1
- submerged_layers: int32 [96, 32], P('region', 'sect'), may hold values from 0 to 128, as said below
- interaction_matrix: float32 [16, 16], replicated, may hold values from -1.5 to 1.5
- bloom_yields: float32 [16], replicated, may hold values from -8 to 8
Outputs:
- tracers_next: float32 [16, 96, 32, 128], P('tracer', 'region', 'sect')
- temperature_next: float32 [96, 32, 128], P('region', 'sect')
Inputs may be any that keep to these rules, and one draw needn't show every extreme that they name: `submerged_layers`: land (0) forms a few contiguous masses, with shallow shelves around them; columns far from land have all 128 levels.
All inputs are finite; a program needn't handle non-finite values.
Results may differ from a plain program's by a relative error of at most 0.0001.
Values sent between devices are 32-bit elements; how exact they have to be, the bound alone decides.
A program may use at most 64 MiB of HBM per device.

v0:
```python
import jax
import jax.numpy as jnp
from jax import lax
from jax.sharding import PartitionSpec as P

STEPS = 3
SUB = 4


TIME_STEP = 0.2
REACT_STEP = 0.1
GROWTH_MAX = 1.0
HALF_SAT = 0.5
WATER_ATT = 3.0
CHL_ATT = 2.0
HEAT_GAIN = 0.5


def padded_2(block, sides, width):
    for axis, dim in sides:
        count = lax.axis_size(axis)
        forward = [(i, i + 1) for i in range(count - 1)]
        forward.append((count - 1, 0))
        backward = [(target, source) for source, target in forward]
        low = lax.ppermute(
            lax.slice_in_dim(block, block.shape[dim] - width, None, axis=dim), axis, forward
        )
        high = lax.ppermute(lax.slice_in_dim(block, 0, width, axis=dim), axis, backward)
        block = jnp.concatenate([low, block, high], axis=dim)
    return block


def face_fluxes(statics):
    speed_h, other_h, wet_h = (statics[0], statics[1], statics[2])
    span_x = wet_h.shape[0] - 2
    span_y = wet_h.shape[1] - 2
    east_flux = (
        speed_h[0 : span_x + 1, 1 : span_y + 1]
        * wet_h[0 : span_x + 1, 1 : span_y + 1]
        * wet_h[1 : span_x + 2, 1 : span_y + 1]
    )
    north_flux = (
        other_h[1 : span_x + 1, 0 : span_y + 1]
        * wet_h[1 : span_x + 1, 0 : span_y + 1]
        * wet_h[1 : span_x + 1, 1 : span_y + 2]
    )
    return (east_flux, north_flux)


def upwind(padded, east_flux, north_flux):
    span_x = padded.shape[1] - 2
    span_y = padded.shape[2] - 2
    flux_x = (
        jnp.maximum(east_flux, 0.0) * padded[:, 0 : span_x + 1, 1 : span_y + 1]
        + jnp.minimum(east_flux, 0.0) * padded[:, 1 : span_x + 2, 1 : span_y + 1]
    )
    flux_y = (
        jnp.maximum(north_flux, 0.0) * padded[:, 1 : span_x + 1, 0 : span_y + 1]
        + jnp.minimum(north_flux, 0.0) * padded[:, 1 : span_x + 1, 1 : span_y + 2]
    )
    return flux_x[:, 1:] - flux_x[:, :-1] + flux_y[:, :, 1:] - flux_y[:, :, :-1]


def light(chl_abs, upper_ones):
    layer_total = chl_abs.shape[-1]
    cells = chl_abs.reshape(-1, layer_total)
    above = jnp.dot(
        cells, upper_ones, precision=lax.Precision.HIGHEST, preferred_element_type=jnp.float32
    )
    above = above.reshape(chl_abs.shape)
    depth = jnp.arange(layer_total, dtype=jnp.float32) + 0.5
    return jnp.exp(
        -(WATER_ATT / layer_total * depth + CHL_ATT / layer_total * (above + 0.5 * chl_abs))
    )


def react(mixture, interaction_matrix, bloom_yields, upper_ones):
    for substep in range(SUB):
        chl_abs = jnp.abs(mixture[1])
        nutrient = mixture[0]
        rate = GROWTH_MAX * light(chl_abs, upper_ones) * nutrient / (jnp.abs(nutrient) + HALF_SAT)
        linear = jnp.einsum(
            "ab,bxyk->axyk", interaction_matrix, mixture, precision=lax.Precision.HIGHEST
        )
        tendency = linear + bloom_yields[:, None, None, None] * (rate * mixture[2])[None]
        mixture = mixture + REACT_STEP * tendency
    chl_abs = jnp.abs(mixture[1])
    heating = HEAT_GAIN * chl_abs * light(chl_abs, upper_ones)
    return (mixture, heating)


def body(
    solute_concentration,
    thermal_anomaly,
    eastward_flow_speed,
    northward_flow_speed,
    submerged_layers,
    interaction_matrix,
    bloom_yields,
):
    layer_total = thermal_anomaly.shape[-1]
    water_mask = (
        lax.broadcasted_iota(jnp.int32, thermal_anomaly.shape, 2) < submerged_layers[:, :, None]
    ).astype(jnp.float32)
    upper_ones = (
        lax.broadcasted_iota(jnp.int32, (layer_total, layer_total), 0)
        < lax.broadcasted_iota(jnp.int32, (layer_total, layer_total), 1)
    ).astype(jnp.float32)
    quarter_rows = water_mask.shape[0] // lax.axis_size("tracer")
    offset = lax.axis_index("tracer") * quarter_rows

    def quarter(field):
        return lax.dynamic_slice_in_dim(field, offset, quarter_rows, 0)

    wet_part = quarter(water_mask)
    statics = padded_2(
        jnp.stack([quarter(eastward_flow_speed), quarter(northward_flow_speed), wet_part]),
        ((("region", "tracer"), 1), ("sect", 2)),
        1,
    )
    east_flux, north_flux = face_fluxes(statics)
    mixture = lax.all_to_all(
        solute_concentration, "tracer", split_axis=1, concat_axis=0, tiled=True
    )
    warming_tendency = quarter(thermal_anomaly)
    for section_index in range(STEPS):
        joined = jnp.concatenate([mixture, warming_tendency[None]], 0)
        padded = padded_2(joined, ((("region", "tracer"), 1), ("sect", 2)), 1)
        advected = wet_part * (joined - TIME_STEP * upwind(padded, east_flux, north_flux))
        mixture, heating = react(advected[:-1], interaction_matrix, bloom_yields, upper_ones)
        warming_tendency = advected[-1] + TIME_STEP * wet_part * heating
    mixture = lax.all_to_all(mixture, "tracer", split_axis=0, concat_axis=1, tiled=True)
    warming_tendency = lax.all_gather(warming_tendency, "tracer", axis=0, tiled=True)
    return (mixture, warming_tendency)


def solution(mesh):
    placed = (
        P("tracer", "region", "sect", None),
        P("region", "sect", None),
        P("region", "sect", None),
        P("region", "sect", None),
        P("region", "sect"),
        P(),
        P(),
    )
    return jax.shard_map(
        body,
        mesh=mesh,
        in_specs=placed,
        out_specs=(P("tracer", "region", "sect", None), P("region", "sect", None)),
        check_vma=False,
    )
```

profile of v0, /device:TPU:0, one launch (start us, length us, event | category | flops | bytes accessed | tf_op | source)
XLA Modules:
  0.0 105.6 jit_solution(13350926067007664395)
XLA Ops:
  2.4 3.0 %collective-permute-start = (f32[3,1,8,128]{3,2,1,0:T(8,128)S(1)}, f32[3,1,8,128]{3,2,1,0:T(8,128)S(1)}, u32[]{:S(2)}, u32[]{:S(2)}) collective-permute-start(f32[3,1,8,128]{3,2,1,0:T(8,128)S(1)} %get-tuple-element.23), channel_id=1, source_target_pairs={{0,4},{4,8},{8,12},{12,16},{16,20},{20,24},{24,28},{28,0},{1,5},{5... | collective-permute-start | bytes 36872 | tf_op jit(solution)/shard_map/ppermute | solution.py:25
  5.4 3.1 %collective-permute-start.1 = (f32[3,1,8,128]{3,2,1,0:T(8,128)S(1)}, f32[3,1,8,128]{3,2,1,0:T(8,128)S(1)}, u32[]{:S(2)}, u32[]{:S(2)}) collective-permute-start(f32[3,1,8,128]{3,2,1,0:T(8,128)S(1)} %get-tuple-element.24), channel_id=1, source_target_pairs={{4,0},{8,4},{12,8},{16,12},{20,16},{24,20},{28,24},{0,28},{5,1},{9... | collective-permute-start | bytes 36872 | tf_op jit(solution)/shard_map/ppermute | solution.py:28
  8.5 2.1 %copy.111 = f32[8,24,8,128]{3,2,0,1:T(8,128)} copy(f32[8,24,8,128]{3,2,1,0:T(8,128)} %param.7) | data formatting | bytes 1572864 | tf_op args[0]
  10.6 3.5 %all-to-all-start = ((f32[8,24,8,128]{3,2,0,1:T(8,128)}), f32[8,24,8,128]{3,2,0,1:T(8,128)S(1)}, u32[]{:S(2)}, u32[]{:S(2)}) async-start(f32[8,24,8,128]{3,2,0,1:T(8,128)} %copy.111), calls=%async_computation | async-start | bytes 1572864 | tf_op jit(solution)/shard_map/all_to_all | solution.py:122
  14.3 1.7 %collective-permute-start.3 = (f32[3,14,1,128]{3,2,1,0:T(1,128)S(1)}, f32[3,14,1,128]{3,2,1,0:T(1,128)S(1)}, u32[]{:S(2)}, u32[]{:S(2)}) collective-permute-start(f32[3,14,1,128]{3,2,1,0:T(1,128)S(1)} %get-tuple-element.22), channel_id=1, source_target_pairs={{1,0},{2,1},{3,2},{0,3},{5,4},{6,5},{7,6},{4,7},{9,8},{10,9},{11,1... | collective-permute-start | bytes 64520 | tf_op jit(solution)/shard_map/ppermute | solution.py:28
  16.0 1.5 %collective-permute-done.2 = f32[3,14,1,128]{3,2,1,0:T(1,128)S(1)} collective-permute-done((f32[3,14,1,128]{3,2,1,0:T(1,128)S(1)}, f32[3,14,1,128]{3,2,1,0:T(1,128)S(1)}, u32[]{:S(2)}, u32[]{:S(2)}) %collective-permute-start.2) | collective-permute-done | bytes 21536 | tf_op jit(solution)/shard_map/ppermute | solution.py:25
  17.7 7.2 %all-to-all-done = f32[8,24,8,128]{3,2,0,1:T(8,128)S(1)} async-done(((f32[8,24,8,128]{3,2,0,1:T(8,128)}), f32[8,24,8,128]{3,2,0,1:T(8,128)S(1)}, u32[]{:S(2)}, u32[]{:S(2)}) %all-to-all-start) | async-done | bytes 786464 | tf_op jit(solution)/shard_map/all_to_all | solution.py:122
  25.4 4.4 %collective-permute-start.5 = (f32[17,1,8,128]{3,2,1,0:T(8,128)S(1)}, f32[17,1,8,128]{3,2,1,0:T(8,128)S(1)}, u32[]{:S(2)}, u32[]{:S(2)}) collective-permute-start(f32[17,1,8,128]{3,2,1,0:T(8,128)S(1)} %get-tuple-element.13), channel_id=1, source_target_pairs={{4,0},{8,4},{12,8},{16,12},{20,16},{24,20},{28,24},{0,28},{5,1},{9... | collective-permute-start | bytes 208904 | tf_op jit(solution)/shard_map/ppermute | solution.py:28
  29.8 2.3 %collective-permute-done.4 = f32[17,1,8,128]{3,2,1,0:T(8,128)S(1)} collective-permute-done((f32[17,1,8,128]{3,2,1,0:T(8,128)S(1)}, f32[17,1,8,128]{3,2,1,0:T(8,128)S(1)}, u32[]{:S(2)}, u32[]{:S(2)}) %collective-permute-start.4) | collective-permute-done | bytes 69664 | tf_op jit(solution)/shard_map/ppermute | solution.py:25
  32.3 1.7 %collective-permute-start.7 = (f32[17,14,1,128]{3,2,1,0:T(1,128)S(1)}, f32[17,14,1,128]{3,2,1,0:T(1,128)S(1)}, u32[]{:S(2)}, u32[]{:S(2)}) collective-permute-start(f32[17,14,1,128]{3,2,1,0:T(1,128)S(1)} %get-tuple-element.7), channel_id=1, source_target_pairs={{1,0},{2,1},{3,2},{0,3},{5,4},{6,5},{7,6},{4,7},{9,8},{10,9},{11,1... | collective-permute-start | bytes 365576 | tf_op jit(solution)/shard_map/ppermute | solution.py:28
  34.1 2.4 %collective-permute-done.6 = f32[17,14,1,128]{3,2,1,0:T(1,128)S(1)} collective-permute-done((f32[17,14,1,128]{3,2,1,0:T(1,128)S(1)}, f32[17,14,1,128]{3,2,1,0:T(1,128)S(1)}, u32[]{:S(2)}, u32[]{:S(2)}) %collective-permute-start.6) | collective-permute-done | bytes 121888 | tf_op jit(solution)/shard_map/ppermute | solution.py:25
  40.1 1.2 %fusion.172 = f32[12,8,128,16]{2,3,1,0:T(8,128)S(1)} fusion(f32[16,12,8,128]{3,2,1,0:T(8,128)S(1)} %fusion.151, f32[16,16]{1,0:T(8,128)S(1)} %copy-done.1), kind=kOutput, calls=%fused_computation.247 | convolution fusion | flops 37748736 | bytes 1573888 | tf_op jit(solution)/shard_map/ab,bxyk->axyk/dot_general | solution.py:82
  41.9 1.2 %fusion.170 = f32[12,8,128,16]{2,3,1,0:T(8,128)S(1)} fusion(f32[16,12,8,128]{3,2,1,0:T(8,128)S(1)} %fusion.149, f32[16,16]{1,0:T(8,128)S(1)} %copy-done.1), kind=kOutput, calls=%fused_computation.245 | convolution fusion | flops 37748736 | bytes 1573888 | tf_op jit(solution)/shard_map/ab,bxyk->axyk/dot_general | solution.py:82
  43.7 1.2 %fusion.168 = f32[12,8,128,16]{2,3,1,0:T(8,128)S(1)} fusion(f32[16,12,8,128]{3,2,1,0:T(8,128)S(1)} %fusion.147, f32[16,16]{1,0:T(8,128)S(1)} %copy-done.1), kind=kOutput, calls=%fused_computation.243 | convolution fusion | flops 37748736 | bytes 1573888 | tf_op jit(solution)/shard_map/ab,bxyk->axyk/dot_general | solution.py:82
  45.5 4.8 %collective-permute-start.9 = (f32[17,1,8,128]{3,2,1,0:T(8,128)S(1)}, f32[17,1,8,128]{3,2,1,0:T(8,128)S(1)}, u32[]{:S(2)}, u32[]{:S(2)}) collective-permute-start(f32[17,1,8,128]{3,2,1,0:T(8,128)S(1)} %get-tuple-element.11), channel_id=1, source_target_pairs={{4,0},{8,4},{12,8},{16,12},{20,16},{24,20},{28,24},{0,28},{5,1},{9... | collective-permute-start | bytes 208904 | tf_op jit(solution)/shard_map/ppermute | solution.py:28
  50.3 2.4 %collective-permute-done.8 = f32[17,1,8,128]{3,2,1,0:T(8,128)S(1)} collective-permute-done((f32[17,1,8,128]{3,2,1,0:T(8,128)S(1)}, f32[17,1,8,128]{3,2,1,0:T(8,128)S(1)}, u32[]{:S(2)}, u32[]{:S(2)}) %collective-permute-start.8) | collective-permute-done | bytes 69664 | tf_op jit(solution)/shard_map/ppermute | solution.py:25
  53.3 1.7 %collective-permute-start.11 = (f32[17,14,1,128]{3,2,1,0:T(1,128)S(1)}, f32[17,14,1,128]{3,2,1,0:T(1,128)S(1)}, u32[]{:S(2)}, u32[]{:S(2)}) collective-permute-start(f32[17,14,1,128]{3,2,1,0:T(1,128)S(1)} %get-tuple-element.5), channel_id=1, source_target_pairs={{1,0},{2,1},{3,2},{0,3},{5,4},{6,5},{7,6},{4,7},{9,8},{10,9},{11,1... | collective-permute-start | bytes 365576 | tf_op jit(solution)/shard_map/ppermute | solution.py:28
  55.1 2.2 %collective-permute-done.10 = f32[17,14,1,128]{3,2,1,0:T(1,128)S(1)} collective-permute-done((f32[17,14,1,128]{3,2,1,0:T(1,128)S(1)}, f32[17,14,1,128]{3,2,1,0:T(1,128)S(1)}, u32[]{:S(2)}, u32[]{:S(2)}) %collective-permute-start.10) | collective-permute-done | bytes 121888 | tf_op jit(solution)/shard_map/ppermute | solution.py:25
  59.2 1.2 %fusion.166 = f32[12,8,128,16]{2,3,1,0:T(8,128)S(1)} fusion(f32[16,12,8,128]{3,2,1,0:T(8,128)S(1)} %slice.419, f32[16,16]{1,0:T(8,128)S(1)} %copy-done.1), kind=kOutput, calls=%fused_computation.241 | convolution fusion | flops 37748736 | bytes 1573888 | tf_op jit(solution)/shard_map/ab,bxyk->axyk/dot_general | solution.py:82
  61.0 1.2 %fusion.164 = f32[12,8,128,16]{2,3,1,0:T(8,128)S(1)} fusion(f32[16,12,8,128]{3,2,1,0:T(8,128)S(1)} %fusion.143, f32[16,16]{1,0:T(8,128)S(1)} %copy-done.1), kind=kOutput, calls=%fused_computation.239 | convolution fusion | flops 37748736 | bytes 1573888 | tf_op jit(solution)/shard_map/ab,bxyk->axyk/dot_general | solution.py:82
  62.8 1.2 %fusion.162 = f32[12,8,128,16]{2,3,1,0:T(8,128)S(1)} fusion(f32[16,12,8,128]{3,2,1,0:T(8,128)S(1)} %fusion.141, f32[16,16]{1,0:T(8,128)S(1)} %copy-done.1), kind=kOutput, calls=%fused_computation.237 | convolution fusion | flops 37748736 | bytes 1573888 | tf_op jit(solution)/shard_map/ab,bxyk->axyk/dot_general | solution.py:82
  64.6 1.2 %fusion.160 = f32[12,8,128,16]{2,3,1,0:T(8,128)S(1)} fusion(f32[16,12,8,128]{3,2,1,0:T(8,128)S(1)} %fusion.139, f32[16,16]{1,0:T(8,128)S(1)} %copy-done.1), kind=kOutput, calls=%fused_computation.235 | convolution fusion | flops 37748736 | bytes 1573888 | tf_op jit(solution)/shard_map/ab,bxyk->axyk/dot_general | solution.py:82
  66.4 4.7 %collective-permute-start.13 = (f32[17,1,8,128]{3,2,1,0:T(8,128)S(1)}, f32[17,1,8,128]{3,2,1,0:T(8,128)S(1)}, u32[]{:S(2)}, u32[]{:S(2)}) collective-permute-start(f32[17,1,8,128]{3,2,1,0:T(8,128)S(1)} %get-tuple-element.9), channel_id=1, source_target_pairs={{4,0},{8,4},{12,8},{16,12},{20,16},{24,20},{28,24},{0,28},{5,1},{9... | collective-permute-start | bytes 208904 | tf_op jit(solution)/shard_map/ppermute | solution.py:28
  71.1 2.6 %collective-permute-done.12 = f32[17,1,8,128]{3,2,1,0:T(8,128)S(1)} collective-permute-done((f32[17,1,8,128]{3,2,1,0:T(8,128)S(1)}, f32[17,1,8,128]{3,2,1,0:T(8,128)S(1)}, u32[]{:S(2)}, u32[]{:S(2)}) %collective-permute-start.12) | collective-permute-done | bytes 69664 | tf_op jit(solution)/shard_map/ppermute | solution.py:25
  74.2 1.5 %collective-permute-start.15 = (f32[17,14,1,128]{3,2,1,0:T(1,128)S(1)}, f32[17,14,1,128]{3,2,1,0:T(1,128)S(1)}, u32[]{:S(2)}, u32[]{:S(2)}) collective-permute-start(f32[17,14,1,128]{3,2,1,0:T(1,128)S(1)} %get-tuple-element.3), channel_id=1, source_target_pairs={{1,0},{2,1},{3,2},{0,3},{5,4},{6,5},{7,6},{4,7},{9,8},{10,9},{11,1... | collective-permute-start | bytes 365576 | tf_op jit(solution)/shard_map/ppermute | solution.py:28
  75.8 2.4 %collective-permute-done.14 = f32[17,14,1,128]{3,2,1,0:T(1,128)S(1)} collective-permute-done((f32[17,14,1,128]{3,2,1,0:T(1,128)S(1)}, f32[17,14,1,128]{3,2,1,0:T(1,128)S(1)}, u32[]{:S(2)}, u32[]{:S(2)}) %collective-permute-start.14) | collective-permute-done | bytes 121888 | tf_op jit(solution)/shard_map/ppermute | solution.py:25
  79.8 1.2 %fusion.158 = f32[12,8,128,16]{2,3,1,0:T(8,128)S(1)} fusion(f32[16,12,8,128]{3,2,1,0:T(8,128)S(1)} %slice.442, f32[16,16]{1,0:T(8,128)S(1)} %copy-done.1), kind=kOutput, calls=%fused_computation.233 | convolution fusion | flops 37748736 | bytes 1573888 | tf_op jit(solution)/shard_map/ab,bxyk->axyk/dot_general | solution.py:82
  81.6 1.2 %fusion.156 = f32[12,8,128,16]{2,3,1,0:T(8,128)S(1)} fusion(f32[16,12,8,128]{3,2,1,0:T(8,128)S(1)} %fusion.135, f32[16,16]{1,0:T(8,128)S(1)} %copy-done.1), kind=kOutput, calls=%fused_computation.231 | convolution fusion | flops 37748736 | bytes 1573888 | tf_op jit(solution)/shard_map/ab,bxyk->axyk/dot_general | solution.py:82
  83.4 1.2 %fusion.154 = f32[12,8,128,16]{2,3,1,0:T(8,128)S(1)} fusion(f32[16,12,8,128]{3,2,1,0:T(8,128)S(1)} %fusion.133, f32[16,16]{1,0:T(8,128)S(1)} %copy-done.1), kind=kOutput, calls=%fused_computation.229 | convolution fusion | flops 37748736 | bytes 1573888 | tf_op jit(solution)/shard_map/ab,bxyk->axyk/dot_general | solution.py:82
  85.2 1.2 %fusion.152 = f32[12,8,128,16]{2,3,1,0:T(8,128)S(1)} fusion(f32[16,12,8,128]{3,2,1,0:T(8,128)S(1)} %fusion.131, f32[16,16]{1,0:T(8,128)S(1)} %copy-done.1), kind=kOutput, calls=%fused_computation.227 | convolution fusion | flops 37748736 | bytes 1573888 | tf_op jit(solution)/shard_map/ab,bxyk->axyk/dot_general | solution.py:82
  87.6 3.5 %all-to-all-start.1 = ((f32[16,12,8,128]{3,2,1,0:T(8,128)}), f32[16,12,8,128]{3,2,1,0:T(8,128)S(1)}, u32[]{:S(2)}, u32[]{:S(2)}) async-start(f32[16,12,8,128]{3,2,1,0:T(8,128)} %fusion.129), calls=%async_computation.1 | async-start | bytes 1572864 | tf_op jit(solution)/shard_map/all_to_all | solution.py:132
  92.2 11.8 %all_gather.3 = f32[24,8,128]{2,1,0:T(8,128)S(1)} all-gather(f32[12,8,128]{2,1,0:T(8,128)S(1)} %fusion.15), channel_id=1, replica_groups=mesh['region'=4,'tracer'=2,'sect'=4] {'tracer'}, dimensions={0}, use_global_device_ids=true | all-gather | bytes 147456 | tf_op jit(solution)/shard_map/all_gather | solution.py:133
  (84 shorter events, 20.1 us)
Async XLA Ops:
  0.6 13.5 %copy-start = (f32[24,8,128]{2,1,0:T(8,128)S(1)}, f32[24,8,128]{2,1,0:T(8,128)}, u32[]{:S(2)}) copy-start(f32[24,8,128]{2,1,0:T(8,128)} %param.8) | copy-start | bytes 294916
  2.4 11.8 %collective-permute-start = (f32[3,1,8,128]{3,2,1,0:T(8,128)S(1)}, f32[3,1,8,128]{3,2,1,0:T(8,128)S(1)}, u32[]{:S(2)}, u32[]{:S(2)}) collective-permute-start(f32[3,1,8,128]{3,2,1,0:T(8,128)S(1)} %get-tuple-element.23), channel_id=1, source_target_pairs={{0,4},{4,8},{8,12},{12,16},{16,20},{20,24},{24,28},{28,0},{1,5},{5... | collective-permute-start | bytes 36872 | tf_op jit(solution)/shard_map/ppermute | solution.py:25
  5.4 8.8 %collective-permute-start.1 = (f32[3,1,8,128]{3,2,1,0:T(8,128)S(1)}, f32[3,1,8,128]{3,2,1,0:T(8,128)S(1)}, u32[]{:S(2)}, u32[]{:S(2)}) collective-permute-start(f32[3,1,8,128]{3,2,1,0:T(8,128)S(1)} %get-tuple-element.24), channel_id=1, source_target_pairs={{4,0},{8,4},{12,8},{16,12},{20,16},{24,20},{28,24},{0,28},{5,1},{9... | collective-permute-start | bytes 36872 | tf_op jit(solution)/shard_map/ppermute | solution.py:28
  10.6 14.3 %all-to-all-start = ((f32[8,24,8,128]{3,2,0,1:T(8,128)}), f32[8,24,8,128]{3,2,0,1:T(8,128)S(1)}, u32[]{:S(2)}, u32[]{:S(2)}) async-start(f32[8,24,8,128]{3,2,0,1:T(8,128)} %copy.111), calls=%async_computation | async-start | bytes 1572864 | tf_op jit(solution)/shard_map/all_to_all | solution.py:122
  14.2 3.3 %collective-permute-start.2 = (f32[3,14,1,128]{3,2,1,0:T(1,128)S(1)}, f32[3,14,1,128]{3,2,1,0:T(1,128)S(1)}, u32[]{:S(2)}, u32[]{:S(2)}) collective-permute-start(f32[3,14,1,128]{3,2,1,0:T(1,128)S(1)} %get-tuple-element.21), channel_id=1, source_target_pairs={{0,1},{1,2},{2,3},{3,0},{4,5},{5,6},{6,7},{7,4},{8,9},{9,10},{10,1... | collective-permute-start | bytes 64520 | tf_op jit(solution)/shard_map/ppermute | solution.py:25
  14.3 3.2 %collective-permute-start.3 = (f32[3,14,1,128]{3,2,1,0:T(1,128)S(1)}, f32[3,14,1,128]{3,2,1,0:T(1,128)S(1)}, u32[]{:S(2)}, u32[]{:S(2)}) collective-permute-start(f32[3,14,1,128]{3,2,1,0:T(1,128)S(1)} %get-tuple-element.22), channel_id=1, source_target_pairs={{1,0},{2,1},{3,2},{0,3},{5,4},{6,5},{7,6},{4,7},{9,8},{10,9},{11,1... | collective-permute-start | bytes 64520 | tf_op jit(solution)/shard_map/ppermute | solution.py:28
  25.0 7.1 %collective-permute-start.4 = (f32[17,1,8,128]{3,2,1,0:T(8,128)S(1)}, f32[17,1,8,128]{3,2,1,0:T(8,128)S(1)}, u32[]{:S(2)}, u32[]{:S(2)}) collective-permute-start(f32[17,1,8,128]{3,2,1,0:T(8,128)S(1)} %get-tuple-element.12), channel_id=1, source_target_pairs={{0,4},{4,8},{8,12},{12,16},{16,20},{20,24},{24,28},{28,0},{1,5},{5... | collective-permute-start | bytes 208904 | tf_op jit(solution)/shard_map/ppermute | solution.py:25
  25.4 6.7 %collective-permute-start.5 = (f32[17,1,8,128]{3,2,1,0:T(8,128)S(1)}, f32[17,1,8,128]{3,2,1,0:T(8,128)S(1)}, u32[]{:S(2)}, u32[]{:S(2)}) collective-permute-start(f32[17,1,8,128]{3,2,1,0:T(8,128)S(1)} %get-tuple-element.13), channel_id=1, source_target_pairs={{4,0},{8,4},{12,8},{16,12},{20,16},{24,20},{28,24},{0,28},{5,1},{9... | collective-permute-start | bytes 208904 | tf_op jit(solution)/shard_map/ppermute | solution.py:28
  32.2 4.3 %collective-permute-start.6 = (f32[17,14,1,128]{3,2,1,0:T(1,128)S(1)}, f32[17,14,1,128]{3,2,1,0:T(1,128)S(1)}, u32[]{:S(2)}, u32[]{:S(2)}) collective-permute-start(f32[17,14,1,128]{3,2,1,0:T(1,128)S(1)} %get-tuple-element.6), channel_id=1, source_target_pairs={{0,1},{1,2},{2,3},{3,0},{4,5},{5,6},{6,7},{7,4},{8,9},{9,10},{10,1... | collective-permute-start | bytes 365576 | tf_op jit(solution)/shard_map/ppermute | solution.py:25
  32.3 4.6 %collective-permute-start.7 = (f32[17,14,1,128]{3,2,1,0:T(1,128)S(1)}, f32[17,14,1,128]{3,2,1,0:T(1,128)S(1)}, u32[]{:S(2)}, u32[]{:S(2)}) collective-permute-start(f32[17,14,1,128]{3,2,1,0:T(1,128)S(1)} %get-tuple-element.7), channel_id=1, source_target_pairs={{1,0},{2,1},{3,2},{0,3},{5,4},{6,5},{7,6},{4,7},{9,8},{10,9},{11,1... | collective-permute-start | bytes 365576 | tf_op jit(solution)/shard_map/ppermute | solution.py:28
  37.6 0.7 copy-start.1
  37.6 1.9 %copy-start.2 = (f32[16]{0:T(128)S(1)}, f32[16]{0:T(128)}, u32[]{:S(2)}) copy-start(f32[16]{0:T(128)} %param.13) | copy-start | bytes 196
  45.5 7.2 %collective-permute-start.8 = (f32[17,1,8,128]{3,2,1,0:T(8,128)S(1)}, f32[17,1,8,128]{3,2,1,0:T(8,128)S(1)}, u32[]{:S(2)}, u32[]{:S(2)}) collective-permute-start(f32[17,1,8,128]{3,2,1,0:T(8,128)S(1)} %get-tuple-element.10), channel_id=1, source_target_pairs={{0,4},{4,8},{8,12},{12,16},{16,20},{20,24},{24,28},{28,0},{1,5},{5... | collective-permute-start | bytes 208904 | tf_op jit(solution)/shard_map/ppermute | solution.py:25
  45.5 7.1 %collective-permute-start.9 = (f32[17,1,8,128]{3,2,1,0:T(8,128)S(1)}, f32[17,1,8,128]{3,2,1,0:T(8,128)S(1)}, u32[]{:S(2)}, u32[]{:S(2)}) collective-permute-start(f32[17,1,8,128]{3,2,1,0:T(8,128)S(1)} %get-tuple-element.11), channel_id=1, source_target_pairs={{4,0},{8,4},{12,8},{16,12},{20,16},{24,20},{28,24},{0,28},{5,1},{9... | collective-permute-start | bytes 208904 | tf_op jit(solution)/shard_map/ppermute | solution.py:28
  52.8 4.5 %collective-permute-start.10 = (f32[17,14,1,128]{3,2,1,0:T(1,128)S(1)}, f32[17,14,1,128]{3,2,1,0:T(1,128)S(1)}, u32[]{:S(2)}, u32[]{:S(2)}) collective-permute-start(f32[17,14,1,128]{3,2,1,0:T(1,128)S(1)} %get-tuple-element.4), channel_id=1, source_target_pairs={{0,1},{1,2},{2,3},{3,0},{4,5},{5,6},{6,7},{7,4},{8,9},{9,10},{10,1... | collective-permute-start | bytes 365576 | tf_op jit(solution)/shard_map/ppermute | solution.py:25
  53.3 4.9 %collective-permute-start.11 = (f32[17,14,1,128]{3,2,1,0:T(1,128)S(1)}, f32[17,14,1,128]{3,2,1,0:T(1,128)S(1)}, u32[]{:S(2)}, u32[]{:S(2)}) collective-permute-start(f32[17,14,1,128]{3,2,1,0:T(1,128)S(1)} %get-tuple-element.5), channel_id=1, source_target_pairs={{1,0},{2,1},{3,2},{0,3},{5,4},{6,5},{7,6},{4,7},{9,8},{10,9},{11,1... | collective-permute-start | bytes 365576 | tf_op jit(solution)/shard_map/ppermute | solution.py:28
  66.4 7.4 %collective-permute-start.12 = (f32[17,1,8,128]{3,2,1,0:T(8,128)S(1)}, f32[17,1,8,128]{3,2,1,0:T(8,128)S(1)}, u32[]{:S(2)}, u32[]{:S(2)}) collective-permute-start(f32[17,1,8,128]{3,2,1,0:T(8,128)S(1)} %get-tuple-element.8), channel_id=1, source_target_pairs={{0,4},{4,8},{8,12},{12,16},{16,20},{20,24},{24,28},{28,0},{1,5},{5... | collective-permute-start | bytes 208904 | tf_op jit(solution)/shard_map/ppermute | solution.py:25
  66.4 7.4 %collective-permute-start.13 = (f32[17,1,8,128]{3,2,1,0:T(8,128)S(1)}, f32[17,1,8,128]{3,2,1,0:T(8,128)S(1)}, u32[]{:S(2)}, u32[]{:S(2)}) collective-permute-start(f32[17,1,8,128]{3,2,1,0:T(8,128)S(1)} %get-tuple-element.9), channel_id=1, source_target_pairs={{4,0},{8,4},{12,8},{16,12},{20,16},{24,20},{28,24},{0,28},{5,1},{9... | collective-permute-start | bytes 208904 | tf_op jit(solution)/shard_map/ppermute | solution.py:28
  73.9 4.3 %collective-permute-start.14 = (f32[17,14,1,128]{3,2,1,0:T(1,128)S(1)}, f32[17,14,1,128]{3,2,1,0:T(1,128)S(1)}, u32[]{:S(2)}, u32[]{:S(2)}) collective-permute-start(f32[17,14,1,128]{3,2,1,0:T(1,128)S(1)} %get-tuple-element.2), channel_id=1, source_target_pairs={{0,1},{1,2},{2,3},{3,0},{4,5},{5,6},{6,7},{7,4},{8,9},{9,10},{10,1... | collective-permute-start | bytes 365576 | tf_op jit(solution)/shard_map/ppermute | solution.py:25
  74.2 4.7 %collective-permute-start.15 = (f32[17,14,1,128]{3,2,1,0:T(1,128)S(1)}, f32[17,14,1,128]{3,2,1,0:T(1,128)S(1)}, u32[]{:S(2)}, u32[]{:S(2)}) collective-permute-start(f32[17,14,1,128]{3,2,1,0:T(1,128)S(1)} %get-tuple-element.3), channel_id=1, source_target_pairs={{1,0},{2,1},{3,2},{0,3},{5,4},{6,5},{7,6},{4,7},{9,8},{10,9},{11,1... | collective-permute-start | bytes 365576 | tf_op jit(solution)/shard_map/ppermute | solution.py:28
  87.6 16.5 %all-to-all-start.1 = ((f32[16,12,8,128]{3,2,1,0:T(8,128)}), f32[16,12,8,128]{3,2,1,0:T(8,128)S(1)}, u32[]{:S(2)}, u32[]{:S(2)}) async-start(f32[16,12,8,128]{3,2,1,0:T(8,128)} %fusion.129), calls=%async_computation.1 | async-start | bytes 1572864 | tf_op jit(solution)/shard_map/all_to_all | solution.py:132
where the time goes:
time: 106 us
  starting transfers between devices  35.1 us (33%)
  waiting for transfers between devices  24.9 us (23%)
  matrix products  18.6 us (18%)
  blocking collectives  11.8 us (11%)
  other arithmetic  7.96 us (8%)
  local copies, waits for them, and re-layouts  6.02 us (6%)
  between operations  1.16 us (1%)
    ppermute x8, starting transfers between devices, padded_2(): lax.ppermute(lax.slice_in_dim(block, 0, width, axis=dim), axis, backward)  23.7 us
    ppermute x8, waiting for transfers between devices, padded_2(): lax.ppermute(lax.slice_in_dim(block, block.shape[dim] - width, None, axis...  15.8 us
    dot_general x12, matrix products, react(): jnp.einsum('ab,bxyk->axyk', interaction_matrix, mixture, precision=lax.Pr...  14.9 us
    all_gather x1, blocking collectives, body(): lax.all_gather(warming_tendency, 'tracer', axis=0, tiled=True)  11.8 us
    all_to_all x1, waiting for transfers between devices, body(): lax.all_to_all(solute_concentration, 'tracer', split_axis=1, concat_axis=...  7.25 us
    add x12, other arithmetic, react(): mixture = mixture + REACT_STEP * tendency  4.89 us
    ppermute x8, starting transfers between devices, padded_2(): lax.ppermute(lax.slice_in_dim(block, block.shape[dim] - width, None, axis...  4.33 us
    unnamed x9, local copies, waits for them, and re-layouts  3.97 us
  transfers between devices with their start and end apart: 18, of which 11 were waited for; matrix products, arithmetic and copies ran while one was open for 3% of the time, Pallas kernels for 0%

commit v1 on v0

v1 whole, which is shorter than its diff:
```python
import functools

import jax
import jax.numpy as jnp
from jax import lax
from jax.experimental import pallas as pl
from jax.experimental.pallas import tpu as pltpu
from jax.sharding import PartitionSpec as P

STEPS = 3
SUB = 4

TIME_STEP = 0.2
REACT_STEP = 0.1
GROWTH_MAX = 1.0
HALF_SAT = 0.5
WATER_ATT = 3.0
CHL_ATT = 2.0
HEAT_GAIN = 0.5

MESH = pl.DeviceIdType.MESH
HIGHEST = lax.Precision.HIGHEST
EAST, WEST, NORTH, SOUTH = range(4)


def iota(shape, dim):
    return lax.broadcasted_iota(jnp.int32, shape, dim)


def exact_dot(a, b, dims=((1,), (0,))):
    return lax.dot_general(
        a, b, (dims, ((), ())), precision=HIGHEST, preferred_element_type=jnp.float32
    )


def halves(x):
    high = x.astype(jnp.bfloat16)
    return high, (x - high.astype(jnp.float32)).astype(jnp.bfloat16)


def half_dot(a, b):
    return jnp.dot(a, b, preferred_element_type=jnp.float32)


def dot3(a, b):
    return half_dot(a[0], b[0]) + half_dot(a[1], b[0]) + half_dot(a[0], b[1])


def tables(rates_ref, yields_ref, tracers, wide, Y):
    rows = tracers * Y
    spread = (iota((rows, tracers), 0) // Y == iota((rows, tracers), 1)).astype(jnp.float32)
    same = iota((rows, rows), 0) % Y == iota((rows, rows), 1) % Y
    full = exact_dot(exact_dot(spread, rates_ref[...]), spread, ((1,), (1,)))
    full = jnp.where(same, full, 0.0) * REACT_STEP
    diagonal = (iota((rows, rows), 0) == iota((rows, rows), 1)).astype(jnp.float32)
    one = diagonal + full
    two = exact_dot(one, one)
    three = exact_dot(two, one)
    four = exact_dot(two, two)
    source = [
        exact_dot(spread * yields_ref[...], jnp.ones((tracers, wide), jnp.float32)) * REACT_STEP
    ]
    for power in (one, two, three):
        source.append(exact_dot(power, source[0]))
    head = jnp.concatenate([power[: 3 * Y] for power in (one, two, three)], axis=0)
    shape = (rows, wide)
    lane = iota(shape, 1)
    inject = jnp.zeros(shape, jnp.float32)
    for sub in range(SUB):
        hit = jnp.logical_and(lane // Y == sub, lane % Y == iota(shape, 0) % Y)
        inject = inject + jnp.where(hit, source[SUB - 1 - sub], 0.0)
    return head, four, inject[:, : SUB * Y], [v[: 3 * Y] for v in source[: SUB - 1]]


def stack(flat, wide):
    return jnp.concatenate(
        [flat[:, i * wide : (i + 1) * wide] for i in range(flat.shape[1] // wide)], axis=0
    )


def unstack(tall, Y):
    return jnp.concatenate(
        [tall[i * Y : (i + 1) * Y] for i in range(tall.shape[0] // Y)], axis=1
    )


def kernel(
    regions, groups, sects,
    solute, heat_in, east_in, north_in, layers_in, rates_ref, yields_ref,
    tracers_out, heat_out,
    state, ysend, yrecv, coef, final,
    in_send, in_recv, halo_send, halo_recv, out_send, out_recv, local_sem,
):
    region, group, sect = (lax.axis_index(a) for a in ("region", "tracer", "sect"))
    own, wide, Y = solute.shape[0], solute.shape[2], layers_in.shape[1]
    tracers = own * groups
    block = heat_in.shape[0] // groups
    span = block // Y
    fields = tracers + 1
    every = fields + 3

    def place(reg, t):
        return t + (reg % 2) * (groups - 1 - 2 * t)

    part = place(region, group)
    last = groups - 1
    next_region = lax.rem(region + 1, regions)
    past_region = lax.rem(region + regions - 1, regions)
    east_region = jnp.where(part == last, next_region, region)
    west_region = jnp.where(part == 0, past_region, region)
    east_part = jnp.where(part == last, 0, part + 1)
    west_part = jnp.where(part == 0, last, part - 1)
    beside = {
        EAST: {"region": east_region, "tracer": place(east_region, east_part)},
        WEST: {"region": west_region, "tracer": place(west_region, west_part)},
        NORTH: {"sect": lax.rem(sect + 1, sects)},
        SOUTH: {"sect": lax.rem(sect + sects - 1, sects)},
    }
    peers = [lax.rem(group + d, groups) for d in range(1, groups)]

    def rows_of(t):
        return pl.ds(pl.multiple_of(place(region, t) * block, Y), block)

    mine = rows_of(group)
    slot = pl.ds(group * own, own)
    inner = pl.ds(Y, block)

    barrier = pltpu.get_barrier_semaphore()
    for peer in peers:
        pl.semaphore_signal(barrier, inc=1, device_id={"tracer": peer}, device_id_type=MESH)
    for side in range(4):
        pl.semaphore_signal(barrier, inc=1, device_id=beside[side], device_id_type=MESH)
    keep = pltpu.make_async_copy(
        solute.at[:, mine, :], state.at[0, slot, inner, :], local_sem.at[0]
    )
    keep.start()
    pl.semaphore_wait(barrier, groups - 1 + 4)

    arriving = []
    for d, peer in enumerate(peers):
        copy = pltpu.make_async_remote_copy(
            src_ref=solute.at[:, rows_of(peer), :],
            dst_ref=state.at[0, slot, inner, :],
            send_sem=in_send.at[d],
            recv_sem=in_recv.at[d],
            device_id={"tracer": peer},
            device_id_type=MESH,
        )
        copy.start()
        arriving.append(copy)

    total = layers_in.shape[0] * Y
    pick = (iota((total, layers_in.shape[0]), 0) // Y == iota((total, layers_in.shape[0]), 1))
    depth = half_dot(
        pick.astype(jnp.bfloat16), layers_in[...].astype(jnp.float32).astype(jnp.bfloat16)
    )
    depth = jnp.where(iota((total, Y), 0) % Y == iota((total, Y), 1), depth, 0.0)
    depth = half_dot(depth.astype(jnp.bfloat16), jnp.ones((Y, wide), jnp.bfloat16))
    coef[5] = (iota((total, wide), 1).astype(jnp.float32) < depth).astype(jnp.float32)
    state[0, tracers, inner, :] = heat_in[mine, :]
    state[0, fields, inner, :] = east_in[mine, :]
    state[0, fields + 1, inner, :] = north_in[mine, :]
    state[0, fields + 2, inner, :] = coef[5, mine, :]

    head, four, inject, source = tables(rates_ref, yields_ref, tracers, wide, Y)
    head, four, inject = halves(head), halves(four), halves(inject)
    upper = (iota((wide, wide), 0) < iota((wide, wide), 1)).astype(jnp.bfloat16)
    level = iota((block, wide), 1).astype(jnp.float32) + 0.5
    tile = (1, span)
    source = [jnp.tile(v, tile) for v in source]

    def light(chl_abs):
        high, low = halves(chl_abs)
        above = half_dot(high, upper) + half_dot(low, upper)
        return jnp.exp(
            -(WATER_ATT / wide * level + CHL_ATT / wide * (above + 0.5 * chl_abs))
        )

    def exchange(step, count):
        some = pl.ds(0, count)
        for f in range(count):
            ysend[step, 0, f] = state[step, f, pl.ds(Y, span, stride=Y), :]
            ysend[step, 1, f] = state[step, f, pl.ds(2 * Y - 1, span, stride=Y), :]
        plan = {
            EAST: (state.at[step, some, pl.ds(block, Y), :], state.at[step, some, pl.ds(0, Y), :]),
            WEST: (
                state.at[step, some, pl.ds(Y, Y), :],
                state.at[step, some, pl.ds(block + Y, Y), :],
            ),
            NORTH: (ysend.at[step, 1, some], yrecv.at[step, 1, some]),
            SOUTH: (ysend.at[step, 0, some], yrecv.at[step, 0, some]),
        }
        copies = []
        for side, (source_ref, target_ref) in plan.items():
            copy = pltpu.make_async_remote_copy(
                src_ref=source_ref,
                dst_ref=target_ref,
                send_sem=halo_send.at[step, side],
                recv_sem=halo_recv.at[step, side],
                device_id=beside[side],
                device_id_type=MESH,
            )
            copy.start()
            copies.append(copy)
        return copies

    def beside_y(step, value, x, first, count):
        at = (count, Y, wide)
        row = iota(at, 1)
        some = pl.ds(first, count)
        above = jnp.broadcast_to(yrecv[step, 0, some, pl.ds(x, 1), :], at)
        below = jnp.broadcast_to(yrecv[step, 1, some, pl.ds(x, 1), :], at)
        up = jnp.where(row == Y - 1, above, pltpu.roll(value, Y - 1, 1))
        down = jnp.where(row == 0, below, pltpu.roll(value, 1, 1))
        return up, down

    keep.wait()
    for copy in arriving:
        copy.wait()

    for step in range(STEPS):
        for copy in exchange(step, every if step == 0 else fields):
            copy.wait()
        columns, heats, wets = [], [], []
        for x in range(span):
            here = pl.ds((x + 1) * Y, Y)
            ahead = pl.ds((x + 2) * Y, Y)
            behind = pl.ds(x * Y, Y)
            cell = pl.ds(x * Y, Y)
            if step == 0:
                speed_wet = state[0, pl.ds(fields + 1, 2), here, :]
                up, down = beside_y(0, speed_wet, x, fields + 1, 2)
                wet = speed_wet[1]
                east = state[0, fields, here, :] * wet * state[0, fields + 2, ahead, :]
                west = state[0, fields, behind, :] * state[0, fields + 2, behind, :] * wet
                north = speed_wet[0] * wet * up[1]
                south = down[0] * down[1] * wet
                scaled = TIME_STEP * wet
                coef[0, cell, :] = wet - scaled * (
                    jnp.maximum(east, 0.0) - jnp.minimum(west, 0.0)
                    + jnp.maximum(north, 0.0) - jnp.minimum(south, 0.0)
                )
                coef[1, cell, :] = -scaled * jnp.minimum(east, 0.0)
                coef[2, cell, :] = scaled * jnp.maximum(west, 0.0)
                coef[3, cell, :] = -scaled * jnp.minimum(north, 0.0)
                coef[4, cell, :] = scaled * jnp.maximum(south, 0.0)
            value = state[step, pl.ds(0, fields), here, :]
            up, down = beside_y(step, value, x, 0, fields)
            moved = (
                coef[0, cell, :] * value
                + coef[1, cell, :] * state[step, pl.ds(0, fields), ahead, :]
                + coef[2, cell, :] * state[step, pl.ds(0, fields), behind, :]
                + coef[3, cell, :] * up
                + coef[4, cell, :] * down
            )
            columns.append(moved[:tracers].reshape(tracers * Y, wide))
            heats.append(moved[tracers])
            wets.append(state[0, fields + 2, here, :])
        mixed = jnp.concatenate(columns, axis=1)
        parts = halves(mixed)
        ahead_rows = dot3(head, parts)
        result = dot3(four, parts)
        rates = []
        for sub in range(SUB):
            if sub == 0:
                rows = mixed[: 3 * Y]
            else:
                rows = ahead_rows[(sub - 1) * 3 * Y : sub * 3 * Y]
                for i, rate in enumerate(rates):
                    rows = rows + source[sub - 1 - i] * jnp.concatenate([rate] * 3, axis=0)
            nutrient, chl, phyto = rows[:Y], rows[Y : 2 * Y], rows[2 * Y :]
            shade = unstack(light(jnp.abs(stack(chl, wide))), Y)
            rates.append(
                GROWTH_MAX * shade * nutrient / (jnp.abs(nutrient) + HALF_SAT) * phyto
            )
        result = result + dot3(inject, halves(jnp.concatenate(rates, axis=0)))
        chl_abs = jnp.abs(stack(result[Y : 2 * Y], wide))
        heating = HEAT_GAIN * chl_abs * light(chl_abs)
        heat = jnp.concatenate(heats, axis=0) + TIME_STEP * jnp.concatenate(wets, axis=0) * heating
        if step < STEPS - 1:
            target, base = state.at[step + 1], Y
        else:
            target, base = final, 0
        for x in range(span):
            target[pl.ds(0, tracers), pl.ds(base + x * Y, Y), :] = result[
                :, x * wide : (x + 1) * wide
            ].reshape(tracers, Y, wide)
        target[tracers, pl.ds(base, block), :] = heat

    leaving = []
    for d, peer in enumerate(peers):
        pairs = (
            (final.at[pl.ds(peer * own, own)], tracers_out.at[:, mine, :]),
            (final.at[tracers], heat_out.at[mine, :]),
        )
        for i, (source_ref, target_ref) in enumerate(pairs):
            copy = pltpu.make_async_remote_copy(
                src_ref=source_ref,
                dst_ref=target_ref,
                send_sem=out_send.at[d, i],
                recv_sem=out_recv.at[d, i],
                device_id={"tracer": peer},
                device_id_type=MESH,
            )
            copy.start()
            leaving.append(copy)
    for i, (source_ref, target_ref) in enumerate(
        ((final.at[slot], tracers_out.at[:, mine, :]), (final.at[tracers], heat_out.at[mine, :]))
    ):
        copy = pltpu.make_async_copy(source_ref, target_ref, local_sem.at[1 + i])
        copy.start()
        leaving.append(copy)
    for copy in leaving:
        copy.wait()


def solution(mesh):
    regions, groups, sects = (mesh.shape[a] for a in ("region", "tracer", "sect"))

    def body(solute, thermal, eastward, northward, layers, rates, yields):
        own, rows, cols, wide = solute.shape
        tracers = own * groups
        span = rows // groups
        fields = tracers + 1
        flat = (rows * cols, wide)
        vmem, hbm = pl.BlockSpec(memory_space=pltpu.VMEM), pl.BlockSpec(memory_space=pl.ANY)
        dma = pltpu.SemaphoreType.DMA
        peers = max(groups - 1, 1)
        mixture, heat = pl.pallas_call(
            functools.partial(kernel, regions, groups, sects),
            out_shape=(
                jax.ShapeDtypeStruct((own, *flat), jnp.float32),
                jax.ShapeDtypeStruct(flat, jnp.float32),
            ),
            in_specs=[hbm] + [vmem] * 6,
            out_specs=(hbm, hbm),
            scratch_shapes=[
                pltpu.VMEM((STEPS, fields + 3, (span + 2) * cols, wide), jnp.float32),
                pltpu.VMEM((STEPS, 2, fields + 3, span, wide), jnp.float32),
                pltpu.VMEM((STEPS, 2, fields + 3, span, wide), jnp.float32),
                pltpu.VMEM((6, *flat), jnp.float32),
                pltpu.VMEM((fields, span * cols, wide), jnp.float32),
                dma((peers,)),
                dma((peers,)),
                dma((STEPS, 4)),
                dma((STEPS, 4)),
                dma((peers, 2)),
                dma((peers, 2)),
                dma((3,)),
            ],
            compiler_params=pltpu.CompilerParams(
                collective_id=0, has_side_effects=True, vmem_limit_bytes=56 << 20
            ),
        )(
            solute.reshape(own, *flat),
            thermal.reshape(flat),
            eastward.reshape(flat),
            northward.reshape(flat),
            layers,
            rates,
            yields.reshape(1, tracers),
        )
        return mixture.reshape(solute.shape), heat.reshape(thermal.shape)

    return jax.shard_map(
        body,
        mesh=mesh,
        in_specs=(
            P("tracer", "region", "sect", None),
            P("region", "sect", None),
            P("region", "sect", None),
            P("region", "sect", None),
            P("region", "sect"),
            P(),
            P(),
        ),
        out_specs=(P("tracer", "region", "sect", None), P("region", "sect", None)),
        check_vma=False,
    )
```

time: 106 us -> 51.2 us (0.48)
  Pallas kernels: 0 us -> 46.2 us
  starting transfers between devices: 35.1 us -> 0 us
  waiting for transfers between devices: 24.9 us -> 0 us
  matrix products: 18.6 us -> 0 us
  blocking collectives: 11.8 us -> 0 us
  other arithmetic: 7.96 us -> 0 us
  local copies, waits for them, and re-layouts: 6.02 us -> 4.1 us
    pallas_call x0 -> x1, Pallas kernels: none -> 46.2 us  [body(): pl.pallas_call(functools.partial(kernel, regions, groups, sects), out_sha...]
    ppermute x16 -> x0, starting transfers between devices: 28 us -> none  [the longest x8 23.7 us: padded_2(): lax.ppermute(lax.slice_in_dim(block, 0, width, axis=dim), axis, backward)]
    dot_general x27 -> x0, matrix products: 18.6 us -> none  [the longest x12 14.9 us: react(): jnp.einsum('ab,bxyk->axyk', interaction_matrix, mixture, precision=lax.Pr...]
    ppermute x16 -> x0, waiting for transfers between devices: 17.7 us -> none  [the longest x8 15.8 us: padded_2(): lax.ppermute(lax.slice_in_dim(block, block.shape[dim] - width, None, axis...]
    all_gather x1 -> x0, blocking collectives: 11.8 us -> none  [body(): lax.all_gather(warming_tendency, 'tracer', axis=0, tiled=True)]
    all_to_all x2 -> x0, waiting for transfers between devices: 7.25 us -> none  [the longest x1 7.25 us: body(): lax.all_to_all(solute_concentration, 'tracer', split_axis=1, concat_axis=...]
    all_to_all x2 -> x0, starting transfers between devices: 7.07 us -> none  [the longest x1 3.54 us: body(): lax.all_to_all(solute_concentration, 'tracer', split_axis=1, concat_axis=...]
    add x18 -> x0, other arithmetic: 6.39 us -> none  [the longest x12 4.89 us: react(): mixture = mixture + REACT_STEP * tendency]
  transfers between devices with their start and end apart: 18 -> 0, of which waited for: 11 -> 0; matrix products, arithmetic and copies ran while one was open for 3% -> 0% of each run, Pallas kernels for 0% -> 0%
where the time goes in v1:
time: 51.2 us; the launch traced here: 51 us
  Pallas kernels  46.2 us (90%)
  local copies, waits for them, and re-layouts  4.1 us (8%)
  between operations  0.66 us (1%)
    pallas_call x1, Pallas kernels, body(): pl.pallas_call(functools.partial(kernel, regions, groups, sects), out_sha...  46.2 us
    unnamed x7, local copies, waits for them, and re-layouts  4.1 us

profile of v1, /device:TPU:0, one launch (start us, length us, event | category | flops | bytes accessed | tf_op | source)
XLA Modules:
  0.0 51.0 jit_solution(13482694968748709397)
XLA Ops:
  0.6 0.0 copy-start.1
  0.6 0.7 %copy-done.1 = s32[24,8]{0,1:T(8,128)S(1)} copy-done((s32[24,8]{0,1:T(8,128)S(1)}, s32[24,8]{0,1:T(8,128)}, u32[]{:S(2)}) %copy-start.1) | copy-done | bytes 792
  1.3 0.7 %copy.9.layers_in = s32[24,8]{1,0:T(8,128)} copy(s32[24,8]{0,1:T(8,128)S(1)} %copy-done.1) | data formatting | bytes 1536 | tf_op args[4]
  2.0 46.2 %shard_map.86 = (f32[8,192,128]{2,1,0:T(8,128)}, f32[192,128]{1,0:T(8,128)}) custom-call(f32[8,192,128]{2,1,0:T(8,128)} %bitcast.8, f32[192,128]{1,0:T(8,128)} %bitcast.10, f32[192,128]{1,0:T(8,128)} %bitcast.11, f32[192,128]{1,0:T(8,128)} %bitcast.12, s32[24,8]{1,0:T(8,128)} %copy.9.layers_in, f32[16,16]{1,0:T(8,128)} %rates_ref.1, f32[1,16]{1,0:T(1,128)} %bitcast.13), custom_call_target="tpu_custom_call" | custom-call | tf_op jit(solution)/shard_map/pallas_call | solution.py:329
  48.2 0.0 copy-start
  48.2 2.1 %copy.12 = f32[8,24,8,128]{3,2,1,0:T(8,128)} copy(f32[8,24,8,128]{3,2,1,0:T(8,128)} %bitcast.7) | data formatting | bytes 1572864
  50.3 0.0 copy-done
  50.3 0.6 %copy.13 = f32[24,8,128]{2,1,0:T(8,128)} copy(f32[24,8,128]{2,1,0:T(8,128)S(1)} %bitcast.9) | data formatting | bytes 196608
Async XLA Ops:
  0.6 0.7 %copy-start.1 = (s32[24,8]{0,1:T(8,128)S(1)}, s32[24,8]{0,1:T(8,128)}, u32[]{:S(2)}) copy-start(s32[24,8]{0,1:T(8,128)} %param.11) | copy-start | bytes 2308
  48.2 2.1 %copy-start = (f32[192,128]{1,0:T(8,128)S(1)}, f32[192,128]{1,0:T(8,128)}, u32[]{:S(2)}) copy-start(f32[192,128]{1,0:T(8,128)} %get-tuple-element.5) | copy-start | bytes 294916

commit v2 on v1

--- a/solution.py
+++ b/solution.py
@@ -84,17 +84,22 @@
     )
 
 
+def plan(span):
+    return (3, (0, 2, 1)) if span % 3 == 0 else (1, (0,))
+
+
 def kernel(
     regions, groups, sects,
-    solute, heat_in, east_in, north_in, layers_in, rates_ref, yields_ref,
+    solute, heat_hbm, east_hbm, north_hbm, layers_hbm, rates_hbm, yields_hbm,
     tracers_out, heat_out,
+    layers_in, rates_ref, yields_ref,
     state, ysend, yrecv, coef, final,
-    in_send, in_recv, halo_send, halo_recv, out_send, out_recv, local_sem,
+    in_send, in_recv, halo_send, halo_recv, out_send, out_recv, local_sem, load_sem,
 ):
     region, group, sect = (lax.axis_index(a) for a in ("region", "tracer", "sect"))
-    own, wide, Y = solute.shape[0], solute.shape[2], layers_in.shape[1]
+    own, wide, Y = solute.shape[0], solute.shape[2], layers_in.shape[0]
     tracers = own * groups
-    block = heat_in.shape[0] // groups
+    block = heat_hbm.shape[0] // groups
     span = block // Y
     fields = tracers + 1
     every = fields + 3
@@ -131,42 +136,66 @@
     for side in range(4):
         pl.semaphore_signal(barrier, inc=1, device_id=beside[side], device_id_type=MESH)
     keep = pltpu.make_async_copy(
-        solute.at[:, mine, :], state.at[0, slot, inner, :], local_sem.at[0]
+        solute.at[:, mine, :], state.at[0, slot, inner, :], local_sem.at[0, 0]
     )
     keep.start()
+    loads = []
+    for i, (source_ref, target_ref) in enumerate(
+        (
+            (layers_hbm, layers_in),
+            (rates_hbm, rates_ref),
+            (yields_hbm, yields_ref),
+            (heat_hbm.at[mine, :], state.at[0, tracers, inner, :]),
+            (east_hbm.at[mine, :], state.at[0, fields, inner, :]),
+            (north_hbm.at[mine, :], state.at[0, fields + 1, inner, :]),
+        )
+    ):
+        copy = pltpu.make_async_copy(source_ref, target_ref, load_sem.at[i])
+        copy.start()
+        loads.append(copy)
     pl.semaphore_wait(barrier, groups - 1 + 4)
 
-    arriving = []
-    for d, peer in enumerate(peers):
-        copy = pltpu.make_async_remote_copy(
-            src_ref=solute.at[:, rows_of(peer), :],
-            dst_ref=state.at[0, slot, inner, :],
-            send_sem=in_send.at[d],
-            recv_sem=in_recv.at[d],
-            device_id={"tracer": peer},
-            device_id_type=MESH,
-        )
-        copy.start()
-        arriving.append(copy)
-
-    total = layers_in.shape[0] * Y
-    pick = (iota((total, layers_in.shape[0]), 0) // Y == iota((total, layers_in.shape[0]), 1))
-    depth = half_dot(
-        pick.astype(jnp.bfloat16), layers_in[...].astype(jnp.float32).astype(jnp.bfloat16)
+    chunks, order = plan(span)
+    deep = span // chunks
+    piece = deep * Y
+
+    def part_of(t, c):
+        return pl.ds(pl.multiple_of(place(region, t) * block + c * piece, Y), piece)
+
+    arriving = {}
+    for i, c in enumerate(order):
+        for d, peer in enumerate(peers):
+            copy = pltpu.make_async_remote_copy(
+                src_ref=solute.at[:, part_of(peer, c), :],
+                dst_ref=state.at[0, slot, pl.ds(Y + c * piece, piece), :],
+                send_sem=in_send.at[d, c],
+                recv_sem=in_recv.at[d, c],
+                device_id={"tracer": peer},
+                device_id_type=MESH,
+            )
+            copy.start()
+            arriving[c, d] = copy
+
+    for copy in loads:
+        copy.wait()
+    total = layers_in.shape[1] * Y
+    pick = (iota((total, layers_in.shape[1]), 0) // Y == iota((total, layers_in.shape[1]), 1))
+    depth = lax.dot_general(
+        pick.astype(jnp.bfloat16),
+        layers_in[...].astype(jnp.float32).astype(jnp.bfloat16),
+        (((1,), (1,)), ((), ())),
+        preferred_element_type=jnp.float32,
     )
     depth = jnp.where(iota((total, Y), 0) % Y == iota((total, Y), 1), depth, 0.0)
     depth = half_dot(depth.astype(jnp.bfloat16), jnp.ones((Y, wide), jnp.bfloat16))
     coef[5] = (iota((total, wide), 1).astype(jnp.float32) < depth).astype(jnp.float32)
-    state[0, tracers, inner, :] = heat_in[mine, :]
-    state[0, fields, inner, :] = east_in[mine, :]
-    state[0, fields + 1, inner, :] = north_in[mine, :]
     state[0, fields + 2, inner, :] = coef[5, mine, :]
 
     head, four, inject, source = tables(rates_ref, yields_ref, tracers, wide, Y)
     head, four, inject = halves(head), halves(four), halves(inject)
     upper = (iota((wide, wide), 0) < iota((wide, wide), 1)).astype(jnp.bfloat16)
-    level = iota((block, wide), 1).astype(jnp.float32) + 0.5
-    tile = (1, span)
+    level = iota((piece, wide), 1).astype(jnp.float32) + 0.5
+    tile = (1, deep)
     source = [jnp.tile(v, tile) for v in source]
 
     def light(chl_abs):
@@ -176,53 +205,100 @@
             -(WATER_ATT / wide * level + CHL_ATT / wide * (above + 0.5 * chl_abs))
         )
 
-    def exchange(step, count):
+    sent = []
+
+    def exchange(step, c):
+        count = every if step == 0 else fields
         some = pl.ds(0, count)
-        for f in range(count):
-            ysend[step, 0, f] = state[step, f, pl.ds(Y, span, stride=Y), :]
-            ysend[step, 1, f] = state[step, f, pl.ds(2 * Y - 1, span, stride=Y), :]
-        plan = {
-            EAST: (state.at[step, some, pl.ds(block, Y), :], state.at[step, some, pl.ds(0, Y), :]),
-            WEST: (
+        moves = {}
+        if c == chunks - 1:
+            moves[EAST] = (
+                state.at[step, some, pl.ds(block, Y), :],
+                state.at[step, some, pl.ds(0, Y), :],
+            )
+        if c == 0:
+            moves[WEST] = (
                 state.at[step, some, pl.ds(Y, Y), :],
                 state.at[step, some, pl.ds(block + Y, Y), :],
-            ),
-            NORTH: (ysend.at[step, 1, some], yrecv.at[step, 1, some]),
-            SOUTH: (ysend.at[step, 0, some], yrecv.at[step, 0, some]),
+            )
+
+        def send(moves):
+            for side, (source_ref, target_ref) in moves.items():
+                copy = pltpu.make_async_remote_copy(
+                    src_ref=source_ref,
+                    dst_ref=target_ref,
+                    send_sem=halo_send.at[step, c, side],
+                    recv_sem=halo_recv.at[step, c, side],
+                    device_id=beside[side],
+                    device_id_type=MESH,
+                )
+                copy.start()
+                sent.append(copy)
+                halos[step, c, side] = copy
+
+        send(moves)
+        for f in range(count):
+            for side, y in ((0, 0), (1, Y - 1)):
+                ysend[step, c, side, f] = state[
+                    step, f, pl.ds(Y + c * piece + y, deep, stride=Y), :
+                ]
+        moves = {
+            NORTH: (ysend.at[step, c, 1, some], yrecv.at[step, c, 1, some]),
+            SOUTH: (ysend.at[step, c, 0, some], yrecv.at[step, c, 0, some]),
         }
-        copies = []
-        for side, (source_ref, target_ref) in plan.items():
-            copy = pltpu.make_async_remote_copy(
-                src_ref=source_ref,
-                dst_ref=target_ref,
-                send_sem=halo_send.at[step, side],
-                recv_sem=halo_recv.at[step, side],
-                device_id=beside[side],
-                device_id_type=MESH,
-            )
-            copy.start()
-            copies.append(copy)
-        return copies
+        send(moves)
+
+    halos = {}
 
     def beside_y(step, value, x, first, count):
         at = (count, Y, wide)
         row = iota(at, 1)
         some = pl.ds(first, count)
-        above = jnp.broadcast_to(yrecv[step, 0, some, pl.ds(x, 1), :], at)
-        below = jnp.broadcast_to(yrecv[step, 1, some, pl.ds(x, 1), :], at)
+        above = jnp.broadcast_to(yrecv[step, x // deep, 0, some, pl.ds(x % deep, 1), :], at)
+        below = jnp.broadcast_to(yrecv[step, x // deep, 1, some, pl.ds(x % deep, 1), :], at)
         up = jnp.where(row == Y - 1, above, pltpu.roll(value, Y - 1, 1))
         down = jnp.where(row == 0, below, pltpu.roll(value, 1, 1))
         return up, down
 
     keep.wait()
-    for copy in arriving:
-        copy.wait()
-
-    for step in range(STEPS):
-        for copy in exchange(step, every if step == 0 else fields):
-            copy.wait()
+    for c in order:
+        for d in range(len(peers)):
+            arriving[c, d].wait_recv()
+        exchange(0, c)
+
+    leaving = []
+
+    def leave(c):
+        rows = pl.ds(c * piece, piece)
+        out_rows = part_of(group, c)
+        for d, peer in enumerate(peers):
+            pairs = (
+                (final.at[pl.ds(peer * own, own), rows, :], tracers_out.at[:, out_rows, :]),
+                (final.at[tracers, rows, :], heat_out.at[out_rows, :]),
+            )
+            for i, (source_ref, target_ref) in enumerate(pairs):
+                copy = pltpu.make_async_remote_copy(
+                    src_ref=source_ref,
+                    dst_ref=target_ref,
+                    send_sem=out_send.at[d, c, i],
+                    recv_sem=out_recv.at[d, c, i],
+                    device_id={"tracer": peer},
+                    device_id_type=MESH,
+                )
+                copy.start()
+                leaving.append(copy)
+        pairs = (
+            (final.at[slot, rows, :], tracers_out.at[:, out_rows, :]),
+            (final.at[tracers, rows, :], heat_out.at[out_rows, :]),
+        )
+        for i, (source_ref, target_ref) in enumerate(pairs):
+            copy = pltpu.make_async_copy(source_ref, target_ref, local_sem.at[c, 1 + i])
+            copy.start()
+            leaving.append(copy)
+
+    def advance(step, c):
         columns, heats, wets = [], [], []
-        for x in range(span):
+        for x in range(c * deep, (c + 1) * deep):
             here = pl.ds((x + 1) * Y, Y)
             ahead = pl.ds((x + 2) * Y, Y)
             behind = pl.ds(x * Y, Y)
@@ -278,40 +354,32 @@
         heating = HEAT_GAIN * chl_abs * light(chl_abs)
         heat = jnp.concatenate(heats, axis=0) + TIME_STEP * jnp.concatenate(wets, axis=0) * heating
         if step < STEPS - 1:
-            target, base = state.at[step + 1], Y
+            target, base = state.at[step + 1], Y + c * piece
         else:
-            target, base = final, 0
-        for x in range(span):
+            target, base = final, c * piece
+        for x in range(deep):
             target[pl.ds(0, tracers), pl.ds(base + x * Y, Y), :] = result[
                 :, x * wide : (x + 1) * wide
             ].reshape(tracers, Y, wide)
-        target[tracers, pl.ds(base, block), :] = heat
-
-    leaving = []
-    for d, peer in enumerate(peers):
-        pairs = (
-            (final.at[pl.ds(peer * own, own)], tracers_out.at[:, mine, :]),
-            (final.at[tracers], heat_out.at[mine, :]),
-        )
-        for i, (source_ref, target_ref) in enumerate(pairs):
-            copy = pltpu.make_async_remote_copy(
-                src_ref=source_ref,
-                dst_ref=target_ref,
-                send_sem=out_send.at[d, i],
-                recv_sem=out_recv.at[d, i],
-                device_id={"tracer": peer},
-                device_id_type=MESH,
-            )
-            copy.start()
-            leaving.append(copy)
-    for i, (source_ref, target_ref) in enumerate(
-        ((final.at[slot], tracers_out.at[:, mine, :]), (final.at[tracers], heat_out.at[mine, :]))
-    ):
-        copy = pltpu.make_async_copy(source_ref, target_ref, local_sem.at[1 + i])
-        copy.start()
-        leaving.append(copy)
+        target[tracers, pl.ds(base, piece), :] = heat
+
+    for step in range(STEPS):
+        for c in order:
+            for side in (NORTH, SOUTH):
+                halos[step, c, side].wait_recv()
+            if c == 0:
+                halos[step, chunks - 1, EAST].wait_recv()
+            if c == chunks - 1:
+                halos[step, 0, WEST].wait_recv()
+            advance(step, c)
+            if step < STEPS - 1:
+                exchange(step + 1, c)
+            else:
+                leave(c)
     for copy in leaving:
         copy.wait()
+    for copy in sent + list(arriving.values()):
+        copy.wait_send()
 
 
 def solution(mesh):
@@ -323,40 +391,45 @@
         span = rows // groups
         fields = tracers + 1
         flat = (rows * cols, wide)
-        vmem, hbm = pl.BlockSpec(memory_space=pltpu.VMEM), pl.BlockSpec(memory_space=pl.ANY)
+        free, hbm = pl.BlockSpec(memory_space=pl.ANY), pl.BlockSpec(memory_space=pltpu.HBM)
         dma = pltpu.SemaphoreType.DMA
         peers = max(groups - 1, 1)
+        chunks = plan(span)[0]
         mixture, heat = pl.pallas_call(
             functools.partial(kernel, regions, groups, sects),
             out_shape=(
                 jax.ShapeDtypeStruct((own, *flat), jnp.float32),
                 jax.ShapeDtypeStruct(flat, jnp.float32),
             ),
-            in_specs=[hbm] + [vmem] * 6,
-            out_specs=(hbm, hbm),
+            in_specs=[hbm] * 7,
+            out_specs=(free, free),
             scratch_shapes=[
+                pltpu.VMEM((cols, rows), jnp.int32),
+                pltpu.VMEM((tracers, tracers), jnp.float32),
+                pltpu.VMEM((1, tracers), jnp.float32),
                 pltpu.VMEM((STEPS, fields + 3, (span + 2) * cols, wide), jnp.float32),
-                pltpu.VMEM((STEPS, 2, fields + 3, span, wide), jnp.float32),
-                pltpu.VMEM((STEPS, 2, fields + 3, span, wide), jnp.float32),
+                pltpu.VMEM((STEPS, chunks, 2, fields + 3, span // chunks, wide), jnp.float32),
+                pltpu.VMEM((STEPS, chunks, 2, fields + 3, span // chunks, wide), jnp.float32),
                 pltpu.VMEM((6, *flat), jnp.float32),
                 pltpu.VMEM((fields, span * cols, wide), jnp.float32),
-                dma((peers,)),
-                dma((peers,)),
-                dma((STEPS, 4)),
-                dma((STEPS, 4)),
-                dma((peers, 2)),
-                dma((peers, 2)),
-                dma((3,)),
+                dma((peers, chunks)),
+                dma((peers, chunks)),
+                dma((STEPS, chunks, 4)),
+                dma((STEPS, chunks, 4)),
+                dma((peers, chunks, 2)),
+                dma((peers, chunks, 2)),
+                dma((chunks, 3)),
+                dma((6,)),
             ],
             compiler_params=pltpu.CompilerParams(
-                collective_id=0, has_side_effects=True, vmem_limit_bytes=56 << 20
+                collective_id=0, has_side_effects=True, vmem_limit_bytes=60 << 20
             ),
         )(
             solute.reshape(own, *flat),
             thermal.reshape(flat),
             eastward.reshape(flat),
             northward.reshape(flat),
-            layers,
+            layers.T,
             rates,
             yields.reshape(1, tracers),
         )

time: 51.2 us -> 46.3 us (0.904)
  Pallas kernels: 46.2 us -> 42.8 us
  local copies, waits for them, and re-layouts: 4.1 us -> 2.75 us
    pallas_call x1, Pallas kernels: 46.2 us -> 42.8 us  [body(): pl.pallas_call(functools.partial(kernel, regions, groups, sects), out_sha...]
    unnamed x7 -> x4, local copies, waits for them, and re-layouts: 4.1 us -> 2.75 us
where the time goes in v2:
time: 46.3 us; the launch traced here: 46.2 us
  Pallas kernels  42.8 us (92%)
  local copies, waits for them, and re-layouts  2.75 us (6%)
  between operations  0.65 us (1%)
    pallas_call x1, Pallas kernels, body(): pl.pallas_call(functools.partial(kernel, regions, groups, sects), out_sha...  42.8 us
    unnamed x4, local copies, waits for them, and re-layouts  2.75 us

profile of v2, /device:TPU:0, one launch (start us, length us, event | category | flops | bytes accessed | tf_op | source)
XLA Modules:
  0.0 46.2 jit_solution(1162214106941470414)
XLA Ops:
  0.6 42.8 %shard_map.86 = (f32[8,192,128]{2,1,0:T(8,128)}, f32[192,128]{1,0:T(8,128)}) custom-call(f32[8,192,128]{2,1,0:T(8,128)} %bitcast.9, f32[192,128]{1,0:T(8,128)} %bitcast.11, f32[192,128]{1,0:T(8,128)} %bitcast.12, f32[192,128]{1,0:T(8,128)} %bitcast.13, s32[8,24]{1,0:T(8,128)} %bitcast.14, f32[16,16]{1,0:T(8,128)} %rates_hbm.1, f32[1,16]{1,0:T(1,128)} %bitcast.15), custom_call_target="tpu_custom_call" | custom-call | tf_op jit(solution)/shard_map/pallas_call | solution.py:398
  43.4 0.0 copy-start
  43.4 2.1 %copy.11 = f32[8,24,8,128]{3,2,1,0:T(8,128)} copy(f32[8,24,8,128]{3,2,1,0:T(8,128)} %bitcast.8) | data formatting | bytes 1572864
  45.5 0.0 copy-done
  45.5 0.6 %copy.12 = f32[24,8,128]{2,1,0:T(8,128)} copy(f32[24,8,128]{2,1,0:T(8,128)S(1)} %bitcast.10) | data formatting | bytes 196608
Async XLA Ops:
  43.4 2.1 %copy-start = (f32[192,128]{1,0:T(8,128)S(1)}, f32[192,128]{1,0:T(8,128)}, u32[]{:S(2)}) copy-start(f32[192,128]{1,0:T(8,128)} %get-tuple-element.5) | copy-start | bytes 294916
